TPU v7x, 512 devices: a whole 4x8x8 slice. The times are simulated.
512 devices in a mesh: doc: 32 (over z_hi, y, core), lab: 16 (over z_lo, x).
Axes of the slice: x: 4, y: 8, z: 8 (z_hi: 2, z_lo: 4; z = z_hi * 4 + z_lo), core: 2. Of those that a mesh axis runs over, the one named last changes fastest.
Arguments:
- embeddings: bfloat16 [262144, 768], P(('doc', 'lab')), may hold values from -6 to 6
- positives: int32 [262144, 16], P(('doc', 'lab')), may hold values from 0 to 16383, as said below
- weights: float32 [131072, 768], P(('doc', 'lab')), may hold values from -6 to 6
- parents: int32 [131072], replicated, may hold values from 0 to 254, as said below
- owners: int32 [4, 32], replicated, may hold values from 0 to 15
- shortlist: int32 [4, 512, 4], replicated, may hold values from 0 to 3, as said below
- counts: int32 [4, 512], replicated, may hold values from 1 to 4, as said below
Outputs:
- trained: float32 [131072, 768], P(('doc', 'lab'))
- momentum: float32 [131072, 768], P(('doc', 'lab'))
Inputs may be any that keep to these rules, and one draw needn't show every extreme that they name: `positives`: each positive code is (s * 16 + j) * 256 + l with s < 4, j < 16, l < 256; repeats allowed. parents[l] is a row of l's own block below l's row; row 0 of a block is its own parent. `shortlist`: the 4 tile numbers of one step and block are distinct. `counts`: in every step some block has all 4 slots live.
All inputs are finite; a program needn't handle non-finite values.
Results may differ from a plain program's by a relative error of at most 0.0003.
Values may be sent and summed in bfloat16 or wider, within the bound.
A program may use at most 64 MiB of HBM per device.

v0:
```python
import jax
import jax.numpy as jnp
from jax import lax
from jax.sharding import PartitionSpec as P

TILE = 128
STEPS = 4
learning_rate = 0.1
beta_rate = 0.9
pull_rate = 1.0


def from_root(value, axis, source):
    kept = jnp.where(lax.axis_index(axis) == source, value, 0).astype(value.dtype)
    return lax.psum(kept, axis)


def from_behind(value, axis, by):
    length = lax.axis_size(axis)
    return lax.ppermute(value, axis, [(i, (i + by) % length) for i in range(length)])


def pick_rows(panel, labels, tiles, tile_rows):
    width = panel.shape[1]
    shaped = panel.reshape(panel.shape[0] // tile_rows, tile_rows, width)
    lshaped = labels.reshape(labels.shape[0] // tile_rows, tile_rows, labels.shape[1])
    rows = jnp.take(shaped, tiles, axis=0).reshape(tiles.shape[0] * tile_rows, width)
    picked = jnp.take(lshaped, tiles, axis=0).reshape(tiles.shape[0] * tile_rows, labels.shape[1])
    return (rows, picked)


def block_update(weight, moment, rows, picked, base, parent_rows, live):
    scale = 1.0 / jnp.sqrt(jnp.float32(rows.shape[1]))
    rows32 = rows.astype(jnp.float32)
    scores = (
        jnp.dot(
            rows32, weight.T, precision=lax.Precision.HIGHEST, preferred_element_type=jnp.float32
        )
        * scale
    )
    label_ids = base + jnp.arange(weight.shape[0], dtype=jnp.int32)
    target = jnp.any(picked[:, :, None] == label_ids[None, None, :], axis=1).astype(jnp.float32)
    resid = (jax.nn.sigmoid(scores) - target) * live[:, None]
    grad = (
        jnp.dot(
            resid.T, rows32, precision=lax.Precision.HIGHEST, preferred_element_type=jnp.float32
        )
        * scale
    )
    grad = grad + pull_rate * (weight - jnp.take(weight, parent_rows, axis=0))
    moment = beta_rate * moment + grad
    return (weight - learning_rate * moment, moment)


def local(embeddings, positives, weights, parents, owners, shortlist, counts):
    doc_index = lax.axis_index("doc")
    lab_index = lax.axis_index("lab")
    doc_count = lax.axis_size("doc")
    lab_count = lax.axis_size("lab")
    block_rows = weights.shape[0]
    tile_rows = TILE
    slots = shortlist.shape[2]
    slot_of_row = jnp.arange(slots * tile_rows, dtype=jnp.int32) // tile_rows
    weight = weights
    moment = jnp.zeros_like(weights)
    for step in range(STEPS):
        root = owners[step, doc_index]
        panel = from_root(embeddings, "lab", root)
        labels = from_root(positives, "lab", root)
        met_block = (doc_index - step) % doc_count * lab_count + lab_index
        if step > 0:
            weight, moment = from_behind((weight, moment), "doc", 1)
        tiles = lax.dynamic_index_in_dim(shortlist[step], met_block, 0, keepdims=False)
        rows, picked = pick_rows(panel, labels, tiles, tile_rows)
        live = (slot_of_row < counts[step, met_block]).astype(jnp.float32)
        parent_rows = lax.dynamic_slice_in_dim(parents, met_block * block_rows, block_rows, 0)
        code_base = (step * lab_count + lab_index) * block_rows
        weight, moment = block_update(weight, moment, rows, picked, code_base, parent_rows, live)
    weight, moment = from_behind((weight, moment), "doc", -(STEPS - 1))
    return (weight, moment)


def solution(mesh):
    return jax.shard_map(
        local,
        mesh=mesh,
        in_specs=(
            P(("doc", "lab"), None),
            P(("doc", "lab"), None),
            P(("doc", "lab"), None),
            P(),
            P(),
            P(),
            P(),
        ),
        out_specs=(P(("doc", "lab"), None), P(("doc", "lab"), None)),
        check_vma=False,
    )
```

profile of v0, /device:TPU:55, one launch (start us, length us, event | category | flops | bytes accessed | tf_op | source)
XLA Modules:
  0.0 590.3 jit_solution(14270951001734933305)
XLA Ops:
  7.2 1.5 constant_dynamic-slice_fusion.5
  11.3 0.8 select_bitcast_fusion
  13.4 2.9 broadcast_select_fusion.4
  17.4 0.8 compare_and_fusion
  18.2 1.1 gather_fusion.2
  19.7 1.5 constant_dynamic-slice_fusion.4
  21.2 0.6 fusion.37
  21.8 0.6 fusion.38
  22.5 0.6 fusion.39
  23.1 0.6 fusion.40
  23.9 144.6 %all-reduce.5.cloned.1.call-done = (s32[4,128,16]{1,2,0:T(8,128)}, s32[4,128,16]{1,2,0:T(8,128)}, s32[4,128,16]{1,2,0:T(8,128)}, s32[4,128,16]{1,2,0:T(8,128)}) async-done(((s32[4,128,16]{1,2,0:T(8,128)}, s32[4,128,16]{1,2,0:T(8,128)}, s32[4,128,16]{1,2,0:T(8,128)}, s32[4,128,16]{1,2,0:T(8,128)}), (s32[4,128,16]{1,2,0:T(8,128)}, s32[4,128,16]{1,2,0:T(8,128)}, s32[4,128,16]{1,2,0:T(8,128)}, ...) | async-done | bytes 131088 | tf_op jit(solution)/shard_map/psum | solution.py:15
  168.5 1.3 gather_fusion.1
  170.1 5.9 compare_reduce_fusion.3
  175.9 175.2 %all-reduce.7.cloned.1.call-done = (bf16[4,128,768]{2,1,0:T(8,128)(2,1)}, bf16[4,128,768]{2,1,0:T(8,128)(2,1)}, bf16[4,128,768]{2,1,0:T(8,128)(2,1)}, bf16[4,128,768]{2,1,0:T(8,128)(2,1)}) async-done(((bf16[4,128,768]{2,1,0:T(8,128)(2,1)}, bf16[4,128,768]{2,1,0:T(8,128)(2,1)}, bf16[4,128,768]{2,1,0:T(8,128)(2,1)}, bf16[4,128,768]{2,1,0:T(8,128)(2,1)}), (bf16[4,128,768]{2,1,0:T(8,128)(2,1)}, ...) | async-done | bytes 3145744 | tf_op jit(solution)/shard_map/psum | solution.py:15
  351.1 1.7 gather_fusion
  353.0 0.9 fusion.24
  354.0 1.8 multiply_subtract_fusion.3
  355.8 12.5 %collective-permute-start = (f32[256,768]{1,0:T(8,128)}, f32[256,768]{1,0:T(8,128)S(1)}, u32[]{:S(2)}, u32[]{:S(2)}) collective-permute-start(f32[256,768]{1,0:T(8,128)} %get-tuple-element.53), channel_id=1, source_target_pairs={{0,16},{16,32},{32,48},{48,64},{64,80},{80,96},{96,112},{112,128},... | collective-permute-start | bytes 2359304 | tf_op jit(solution)/shard_map/ppermute | solution.py:20
  369.1 5.9 compare_reduce_fusion.2
  375.0 1.7 gather_fusion.3
  376.8 1.9 collective-permute-start.1
  378.9 1.1 gather_fusion.5
  380.0 0.9 fusion.22
  380.9 0.9 convolution_multiply_fusion.2
  381.8 5.8 collective-permute-done.1
  387.6 2.3 multiply_subtract_fusion.2
  389.9 4.6 collective-permute-start.2
  395.4 5.9 compare_reduce_fusion.1
  401.9 15.6 %collective-permute-start.3 = (f32[256,768]{1,0:T(8,128)S(1)}, f32[256,768]{1,0:T(8,128)}, u32[]{:S(2)}, u32[]{:S(2)}) collective-permute-start(f32[256,768]{1,0:T(8,128)S(1)} %get-tuple-element.22), channel_id=1, source_target_pairs={{0,16},{16,32},{32,48},{48,64},{64,80},{80,96},{96,112},{112,128},... | collective-permute-start | bytes 2359304 | tf_op jit(solution)/shard_map/ppermute | solution.py:20
  417.6 1.1 gather_fusion.8
  418.7 0.9 fusion.20
  419.7 0.9 convolution_multiply_fusion.1
  420.6 5.6 collective-permute-done.3
  426.2 2.3 multiply_subtract_fusion.1
  428.5 7.3 %collective-permute-start.4 = (f32[256,768]{1,0:T(8,128)}, f32[256,768]{1,0:T(8,128)S(1)}, u32[]{:S(2)}, u32[]{:S(2)}) collective-permute-start(f32[256,768]{1,0:T(8,128)} %get-tuple-element.17), channel_id=1, source_target_pairs={{0,16},{16,32},{32,48},{48,64},{64,80},{80,96},{96,112},{112,128},... | collective-permute-start | bytes 2359304 | tf_op jit(solution)/shard_map/ppermute | solution.py:20
  436.7 5.9 compare_reduce_fusion
  443.2 22.2 %collective-permute-start.5 = (f32[256,768]{1,0:T(8,128)S(1)}, f32[256,768]{1,0:T(8,128)}, u32[]{:S(2)}, u32[]{:S(2)}) collective-permute-start(f32[256,768]{1,0:T(8,128)S(1)} %get-tuple-element.18), channel_id=1, source_target_pairs={{0,16},{16,32},{32,48},{48,64},{64,80},{80,96},{96,112},{112,128},... | collective-permute-start | bytes 2359304 | tf_op jit(solution)/shard_map/ppermute | solution.py:20
  465.6 1.1 gather_fusion.11
  466.7 0.9 fusion.18
  467.6 0.9 convolution_multiply_fusion
  468.5 5.8 collective-permute-done.5
  474.3 1.4 multiply_subtract_fusion
  475.8 1.9 collective-permute-start.6
  477.7 1.9 collective-permute-start.7
  479.6 87.9 %collective-permute-done.6 = f32[256,768]{1,0:T(8,128)S(1)} collective-permute-done((f32[256,768]{1,0:T(8,128)S(1)}, f32[256,768]{1,0:T(8,128)S(1)}, u32[]{:S(2)}, u32[]{:S(2)}) %collective-permute-start.6) | collective-permute-done | bytes 786464 | tf_op jit(solution)/shard_map/ppermute | solution.py:20
  567.5 14.3 %collective-permute-done.7 = f32[256,768]{1,0:T(8,128)S(1)} collective-permute-done((f32[256,768]{1,0:T(8,128)S(1)}, f32[256,768]{1,0:T(8,128)S(1)}, u32[]{:S(2)}, u32[]{:S(2)}) %collective-permute-start.7) | collective-permute-done | bytes 786464 | tf_op jit(solution)/shard_map/ppermute | solution.py:20
  581.7 0.9 copy.63
  582.6 0.9 copy.64
  (61 shorter events, 7.1 us)
Async XLA Ops:
  7.2 161.4 %all-reduce.5.cloned.1.call-start = ((), (), s32[]{:S(2)}) async-start(), calls=%async_computation | async-start | bytes 262144 | tf_op jit(solution)/shard_map/psum | solution.py:15
  13.3 337.8 %all-reduce.7.cloned.1.call-start = ((), (), s32[]{:S(2)}) async-start(), calls=%async_computation.1 | async-start | bytes 6291456 | tf_op jit(solution)/shard_map/psum | solution.py:15
  16.2 0.8 copy-start.6
  16.2 2.0 copy-start
  354.0 14.4 %copy-start.3 = (s32[4,128,16]{1,2,0:T(8,128)S(1)}, s32[4,128,16]{1,2,0:T(8,128)}, u32[]{:S(2)}) copy-start(s32[4,128,16]{1,2,0:T(8,128)} %get-tuple-element.6) | copy-start | bytes 98308
  355.8 23.0 %collective-permute-start = (f32[256,768]{1,0:T(8,128)}, f32[256,768]{1,0:T(8,128)S(1)}, u32[]{:S(2)}, u32[]{:S(2)}) collective-permute-start(f32[256,768]{1,0:T(8,128)} %get-tuple-element.53), channel_id=1, source_target_pairs={{0,16},{16,32},{32,48},{48,64},{64,80},{80,96},{96,112},{112,128},... | collective-permute-start | bytes 2359304 | tf_op jit(solution)/shard_map/ppermute | solution.py:20
  376.8 10.8 %collective-permute-start.1 = (f32[256,768]{1,0:T(8,128)S(1)}, f32[256,768]{1,0:T(8,128)}, u32[]{:S(2)}, u32[]{:S(2)}) collective-permute-start(f32[256,768]{1,0:T(8,128)S(1)} %get-tuple-element.54), channel_id=1, source_target_pairs={{0,16},{16,32},{32,48},{48,64},{64,80},{80,96},{96,112},{112,128},... | collective-permute-start | bytes 2359304 | tf_op jit(solution)/shard_map/ppermute | solution.py:20
  387.6 7.0 %copy-start.2 = (s32[4,128,16]{1,2,0:T(8,128)S(1)}, s32[4,128,16]{1,2,0:T(8,128)}, u32[]{:S(2)}) copy-start(s32[4,128,16]{1,2,0:T(8,128)} %get-tuple-element.7) | copy-start | bytes 98308
  389.9 11.3 %copy-start.5 = (bf16[4,128,768]{2,1,0:T(8,128)(2,1)S(1)}, bf16[4,128,768]{2,1,0:T(8,128)(2,1)}, u32[]{:S(2)}) copy-start(bf16[4,128,768]{2,1,0:T(8,128)(2,1)} %get-tuple-element.11) | copy-start | bytes 2359300
  389.9 27.7 %collective-permute-start.2 = (f32[256,768]{1,0:T(8,128)}, f32[256,768]{1,0:T(8,128)S(1)}, u32[]{:S(2)}, u32[]{:S(2)}) collective-permute-start(f32[256,768]{1,0:T(8,128)} %get-tuple-element.21), channel_id=1, source_target_pairs={{0,16},{16,32},{32,48},{48,64},{64,80},{80,96},{96,112},{112,128},... | collective-permute-start | bytes 2359304 | tf_op jit(solution)/shard_map/ppermute | solution.py:20
  401.9 24.3 %collective-permute-start.3 = (f32[256,768]{1,0:T(8,128)S(1)}, f32[256,768]{1,0:T(8,128)}, u32[]{:S(2)}, u32[]{:S(2)}) collective-permute-start(f32[256,768]{1,0:T(8,128)S(1)} %get-tuple-element.22), channel_id=1, source_target_pairs={{0,16},{16,32},{32,48},{48,64},{64,80},{80,96},{96,112},{112,128},... | collective-permute-start | bytes 2359304 | tf_op jit(solution)/shard_map/ppermute | solution.py:20
  426.2 9.7 %copy-start.1 = (s32[4,128,16]{1,2,0:T(8,128)S(1)}, s32[4,128,16]{1,2,0:T(8,128)}, u32[]{:S(2)}) copy-start(s32[4,128,16]{1,2,0:T(8,128)} %get-tuple-element.8) | copy-start | bytes 98308
  428.5 14.0 %copy-start.4 = (bf16[4,128,768]{2,1,0:T(8,128)(2,1)S(1)}, bf16[4,128,768]{2,1,0:T(8,128)(2,1)}, u32[]{:S(2)}) copy-start(bf16[4,128,768]{2,1,0:T(8,128)(2,1)} %get-tuple-element.12) | copy-start | bytes 2359300
  428.5 37.0 %collective-permute-start.4 = (f32[256,768]{1,0:T(8,128)}, f32[256,768]{1,0:T(8,128)S(1)}, u32[]{:S(2)}, u32[]{:S(2)}) collective-permute-start(f32[256,768]{1,0:T(8,128)} %get-tuple-element.17), channel_id=1, source_target_pairs={{0,16},{16,32},{32,48},{48,64},{64,80},{80,96},{96,112},{112,128},... | collective-permute-start | bytes 2359304 | tf_op jit(solution)/shard_map/ppermute | solution.py:20
  443.2 31.1 %collective-permute-start.5 = (f32[256,768]{1,0:T(8,128)S(1)}, f32[256,768]{1,0:T(8,128)}, u32[]{:S(2)}, u32[]{:S(2)}) collective-permute-start(f32[256,768]{1,0:T(8,128)S(1)} %get-tuple-element.18), channel_id=1, source_target_pairs={{0,16},{16,32},{32,48},{48,64},{64,80},{80,96},{96,112},{112,128},... | collective-permute-start | bytes 2359304 | tf_op jit(solution)/shard_map/ppermute | solution.py:20
  475.8 91.7 %collective-permute-start.6 = (f32[256,768]{1,0:T(8,128)S(1)}, f32[256,768]{1,0:T(8,128)S(1)}, u32[]{:S(2)}, u32[]{:S(2)}) collective-permute-start(f32[256,768]{1,0:T(8,128)S(1)} %get-tuple-element.13), channel_id=1, source_target_pairs={{0,464},{16,480},{32,496},{48,0},{64,16},{80,32},{96,48},{112,64},... | collective-permute-start | bytes 2359304 | tf_op jit(solution)/shard_map/ppermute | solution.py:20
  477.7 104.1 %collective-permute-start.7 = (f32[256,768]{1,0:T(8,128)S(1)}, f32[256,768]{1,0:T(8,128)S(1)}, u32[]{:S(2)}, u32[]{:S(2)}) collective-permute-start(f32[256,768]{1,0:T(8,128)S(1)} %get-tuple-element.14), channel_id=1, source_target_pairs={{0,464},{16,480},{32,496},{48,0},{64,16},{80,32},{96,48},{112,64},... | collective-permute-start | bytes 2359304 | tf_op jit(solution)/shard_map/ppermute | solution.py:20
Sparse Core Ops, SparseCore 0:
  13.4 155.0 all-reduce.4
  172.6 178.4 all-reduce.6
where the time goes:
time: 591 us; the launch traced here: 590 us
  waiting for transfers between devices  439 us (74%)
  starting transfers between devices  68.1 us (12%)
  other arithmetic  37.6 us (6%)
  local copies, waits for them, and re-layouts  19.8 us (3%)
  between operations  17.3 us (3%)
  matrix products  8.22 us (1%)
    psum x2, waiting for transfers between devices, from_root(): return lax.psum(kept, axis)  320 us
    ppermute x8, waiting for transfers between devices, from_behind(): lax.ppermute(value, axis, [(i, (i + by) % length) for i in range(length)])  119 us
    ppermute x8, starting transfers between devices, from_behind(): lax.ppermute(value, axis, [(i, (i + by) % length) for i in range(length)])  68 us
    reduce_or x4, other arithmetic, block_update(): jnp.any(picked[:, :, None] == label_ids[None, None, :], axis=1)  23.6 us
  transfers between devices with their start and end apart: 10, of which 7 were waited for; matrix products, arithmetic and copies ran while one was open for 8% of the time, Pallas kernels for 0%

commit v1 on v0

--- a/solution.py
+++ b/solution.py
@@ -12,7 +12,7 @@
 
 def from_root(value, axis, source):
     kept = jnp.where(lax.axis_index(axis) == source, value, 0).astype(value.dtype)
-    return lax.psum(kept, axis)
+    return jnp.sum(lax.all_gather(kept, axis), axis=0)
 
 
 def from_behind(value, axis, by):

time: 591 us -> 819 us (1.39)
  blocking collectives: 0 us -> 162 us
  waiting for transfers between devices: 439 us -> 502 us
  other arithmetic: 37.6 us -> 66.2 us
  starting transfers between devices: 68.1 us -> 46 us
    all_gather x0 -> x4, waiting for transfers between devices: none -> 369 us  [from_root(): return jnp.sum(lax.all_gather(kept, axis), axis=0)]
    psum x2 -> x0, waiting for transfers between devices: 320 us -> none  [from_root(): return lax.psum(kept, axis)]
    all_gather x0 -> x4, blocking collectives: none -> 162 us  [from_root(): return jnp.sum(lax.all_gather(kept, axis), axis=0)]
    reduce_sum x0 -> x8, other arithmetic: none -> 27.7 us  [from_root(): return jnp.sum(lax.all_gather(kept, axis), axis=0)]
    ppermute x8, starting transfers between devices: 68 us -> 45.8 us  [from_behind(): lax.ppermute(value, axis, [(i, (i + by) % length) for i in range(length)])]
    ppermute x8, waiting for transfers between devices: 119 us -> 131 us  [from_behind(): lax.ppermute(value, axis, [(i, (i + by) % length) for i in range(length)])]
  transfers between devices with their start and end apart: 10 -> 12, of which waited for: 7 -> 8; matrix products, arithmetic and copies ran while one was open for 8% -> 10% of each run, Pallas kernels for 0% -> 0%
where the time goes in v1:
time: 819 us; the launch traced here: 818 us
  waiting for transfers between devices  502 us (61%)
  blocking collectives  162 us (20%)
  other arithmetic  66.2 us (8%)
  starting transfers between devices  46 us (6%)
  between operations  17.1 us (2%)
  local copies, waits for them, and re-layouts  16.9 us (2%)
  matrix products  8.24 us (1%)
    all_gather x4, waiting for transfers between devices, from_root(): return jnp.sum(lax.all_gather(kept, axis), axis=0)  369 us
    all_gather x4, blocking collectives, from_root(): return jnp.sum(lax.all_gather(kept, axis), axis=0)  162 us
    ppermute x8, waiting for transfers between devices, from_behind(): lax.ppermute(value, axis, [(i, (i + by) % length) for i in range(length)])  131 us
    ppermute x8, starting transfers between devices, from_behind(): lax.ppermute(value, axis, [(i, (i + by) % length) for i in range(length)])  45.8 us
    reduce_sum x8, other arithmetic, from_root(): return jnp.sum(lax.all_gather(kept, axis), axis=0)  27.7 us
    reduce_or x4, other arithmetic, block_update(): jnp.any(picked[:, :, None] == label_ids[None, None, :], axis=1)  24.5 us
  transfers between devices with their start and end apart: 12, of which 8 were waited for; matrix products, arithmetic and copies ran while one was open for 10% of the time, Pallas kernels for 0%

profile of v1, /device:TPU:55, one launch (start us, length us, event | category | flops | bytes accessed | tf_op | source)
XLA Modules:
  0.0 818.4 jit_solution(11423930810545539306)
XLA Ops:
  7.2 1.5 constant_dynamic-slice_fusion.5
  11.3 2.9 broadcast_select_fusion.4
  17.1 37.2 %all-gather.1 = s32[8192,16]{0,1:T(8,128)S(1)} all-gather(s32[512,16]{0,1:T(8,128)S(1)} %get-tuple-element.31), channel_id=3, replica_groups=mesh['doc'=32,'lab'=16] {'lab'}, dimensions={0}, use_global_device_ids=true | all-gather | bytes 557056 | tf_op jit(solution)/shard_map/all_gather | solution.py:15
  56.6 46.3 %all-gather.3 = s32[8192,16]{0,1:T(8,128)S(1)} all-gather(s32[512,16]{0,1:T(8,128)S(1)} %get-tuple-element.30), channel_id=5, replica_groups=mesh['doc'=32,'lab'=16] {'lab'}, dimensions={0}, use_global_device_ids=true | all-gather | bytes 557056 | tf_op jit(solution)/shard_map/all_gather | solution.py:15
  103.2 39.3 %all-gather.5 = s32[8192,16]{0,1:T(8,128)S(1)} all-gather(s32[512,16]{0,1:T(8,128)S(1)} %get-tuple-element.32), channel_id=7, replica_groups=mesh['doc'=32,'lab'=16] {'lab'}, dimensions={0}, use_global_device_ids=true | all-gather | bytes 557056 | tf_op jit(solution)/shard_map/all_gather | solution.py:15
  142.8 39.3 %all-gather.7 = s32[8192,16]{0,1:T(8,128)S(1)} all-gather(s32[512,16]{0,1:T(8,128)S(1)} %get-tuple-element.29), channel_id=9, replica_groups=mesh['doc'=32,'lab'=16] {'lab'}, dimensions={0}, use_global_device_ids=true | all-gather | bytes 557056 | tf_op jit(solution)/shard_map/all_gather | solution.py:15
  183.3 1.1 gather_fusion.2
  185.5 1.5 constant_dynamic-slice_fusion.4
  189.3 6.8 compare_reduce_fusion.3
  196.2 7.0 reduce_sum.84
  204.0 0.9 fusion.24
  204.9 1.9 multiply_subtract_fusion.3
  206.8 19.7 %collective-permute-start = (f32[256,768]{1,0:T(8,128)}, f32[256,768]{1,0:T(8,128)S(1)}, u32[]{:S(2)}, u32[]{:S(2)}) collective-permute-start(f32[256,768]{1,0:T(8,128)} %get-tuple-element.45), channel_id=1, source_target_pairs={{0,16},{16,32},{32,48},{48,64},{64,80},{80,96},{96,112},{112,128},... | collective-permute-start | bytes 2359304 | tf_op jit(solution)/shard_map/ppermute | solution.py:20
  227.3 5.9 compare_reduce_fusion.2
  233.2 92.7 %all-gather.15.cloned.1.call-done = bf16[8192,768]{1,0:T(8,128)(2,1)} async-done(((bf16[512,768]{1,0:T(8,128)(2,1)}), bf16[8192,768]{1,0:T(8,128)(2,1)}) %all-gather.15.cloned.1.call-update) | async-done | bytes 12582928 | tf_op jit(solution)/shard_map/all_gather | solution.py:15
  325.9 6.8 reduce_sum.86
  333.3 2.8 collective-permute-start.1
  336.2 1.1 gather_fusion.5
  337.3 0.9 fusion.22
  338.3 0.9 convolution_multiply_fusion.2
  339.2 5.8 collective-permute-done.1
  345.0 2.3 multiply_subtract_fusion.2
  347.3 4.5 collective-permute-start.2
  352.6 5.9 compare_reduce_fusion.1
  358.5 130.9 %all-gather.17.cloned.1.call-done = bf16[8192,768]{1,0:T(8,128)(2,1)} async-done(((bf16[512,768]{1,0:T(8,128)(2,1)}), bf16[8192,768]{1,0:T(8,128)(2,1)}) %all-gather.17.cloned.1.call-update) | async-done | bytes 12582928 | tf_op jit(solution)/shard_map/all_gather | solution.py:15
  489.3 6.8 reduce_sum.88
  496.7 3.1 collective-permute-start.3
  499.9 1.1 gather_fusion.8
  501.0 0.9 fusion.20
  502.0 0.9 convolution_multiply_fusion.1
  502.8 5.6 collective-permute-done.3
  508.5 2.3 multiply_subtract_fusion.1
  510.8 4.5 collective-permute-start.4
  516.0 5.9 compare_reduce_fusion
  521.9 145.5 %all-gather.19.cloned.1.call-done = bf16[8192,768]{1,0:T(8,128)(2,1)} async-done(((bf16[512,768]{1,0:T(8,128)(2,1)}), bf16[8192,768]{1,0:T(8,128)(2,1)}) %all-gather.19.cloned.1.call-update) | async-done | bytes 12582928 | tf_op jit(solution)/shard_map/all_gather | solution.py:15
  667.4 6.8 reduce_sum.90
  674.8 2.8 collective-permute-start.5
  677.8 1.1 gather_fusion.11
  678.9 0.9 fusion.18
  679.8 0.9 convolution_multiply_fusion
  680.7 5.8 collective-permute-done.5
  686.5 1.4 multiply_subtract_fusion
  688.0 5.3 collective-permute-start.6
  693.3 3.2 collective-permute-start.7
  696.5 99.6 %collective-permute-done.6 = f32[256,768]{1,0:T(8,128)S(1)} collective-permute-done((f32[256,768]{1,0:T(8,128)S(1)}, f32[256,768]{1,0:T(8,128)S(1)}, u32[]{:S(2)}, u32[]{:S(2)}) %collective-permute-start.6) | collective-permute-done | bytes 786464 | tf_op jit(solution)/shard_map/ppermute | solution.py:20
  796.1 14.0 %collective-permute-done.7 = f32[256,768]{1,0:T(8,128)S(1)} collective-permute-done((f32[256,768]{1,0:T(8,128)S(1)}, f32[256,768]{1,0:T(8,128)S(1)}, u32[]{:S(2)}, u32[]{:S(2)}) %collective-permute-start.7) | collective-permute-done | bytes 786464 | tf_op jit(solution)/shard_map/ppermute | solution.py:20
  810.1 0.9 copy.59
  811.0 0.9 copy.60
  (77 shorter events, 15.4 us)
Async XLA Ops:
  7.2 47.5 %copy-start.1 = (s32[4,512,4]{1,2,0:T(4,128)S(1)}, s32[4,512,4]{1,2,0:T(4,128)}, u32[]{:S(2)}) copy-start(s32[4,512,4]{1,2,0:T(4,128)} %param.18) | copy-start | bytes 98308
  7.2 176.1 %copy-start = (f32[256,768]{1,0:T(8,128)S(1)}, f32[256,768]{1,0:T(8,128)}, u32[]{:S(2)}) copy-start(f32[256,768]{1,0:T(8,128)} %param.15) | copy-start | bytes 2359300
  7.2 189.0 %all-gather.13.cloned.1.call-start = ((), (), s32[]{:S(2)}) async-start(), calls=%async_computation | async-start | bytes 13369344 | tf_op jit(solution)/shard_map/all_gather | solution.py:15
  14.2 311.7 %all-gather.15.cloned.1.call-start = ((), (), s32[]{:S(2)}) async-start(), calls=%async_computation.1 | async-start | bytes 13369344 | tf_op jit(solution)/shard_map/all_gather | solution.py:15
  14.9 474.4 %all-gather.17.cloned.1.call-start = ((), (), s32[]{:S(2)}) async-start(), calls=%async_computation.2 | async-start | bytes 13369344 | tf_op jit(solution)/shard_map/all_gather | solution.py:15
  15.7 651.8 %all-gather.19.cloned.1.call-start = ((), (), s32[]{:S(2)}) async-start(), calls=%async_computation.3 | async-start | bytes 13369344 | tf_op jit(solution)/shard_map/all_gather | solution.py:15
  206.8 129.5 %collective-permute-start = (f32[256,768]{1,0:T(8,128)}, f32[256,768]{1,0:T(8,128)S(1)}, u32[]{:S(2)}, u32[]{:S(2)}) collective-permute-start(f32[256,768]{1,0:T(8,128)} %get-tuple-element.45), channel_id=1, source_target_pairs={{0,16},{16,32},{32,48},{48,64},{64,80},{80,96},{96,112},{112,128},... | collective-permute-start | bytes 2359304 | tf_op jit(solution)/shard_map/ppermute | solution.py:20
  333.3 11.7 %collective-permute-start.1 = (f32[256,768]{1,0:T(8,128)S(1)}, f32[256,768]{1,0:T(8,128)}, u32[]{:S(2)}, u32[]{:S(2)}) collective-permute-start(f32[256,768]{1,0:T(8,128)S(1)} %get-tuple-element.46), channel_id=1, source_target_pairs={{0,16},{16,32},{32,48},{48,64},{64,80},{80,96},{96,112},{112,128},... | collective-permute-start | bytes 2359304 | tf_op jit(solution)/shard_map/ppermute | solution.py:20
  347.3 152.6 %collective-permute-start.2 = (f32[256,768]{1,0:T(8,128)}, f32[256,768]{1,0:T(8,128)S(1)}, u32[]{:S(2)}, u32[]{:S(2)}) collective-permute-start(f32[256,768]{1,0:T(8,128)} %get-tuple-element.13), channel_id=1, source_target_pairs={{0,16},{16,32},{32,48},{48,64},{64,80},{80,96},{96,112},{112,128},... | collective-permute-start | bytes 2359304 | tf_op jit(solution)/shard_map/ppermute | solution.py:20
  496.7 11.8 %collective-permute-start.3 = (f32[256,768]{1,0:T(8,128)S(1)}, f32[256,768]{1,0:T(8,128)}, u32[]{:S(2)}, u32[]{:S(2)}) collective-permute-start(f32[256,768]{1,0:T(8,128)S(1)} %get-tuple-element.14), channel_id=1, source_target_pairs={{0,16},{16,32},{32,48},{48,64},{64,80},{80,96},{96,112},{112,128},... | collective-permute-start | bytes 2359304 | tf_op jit(solution)/shard_map/ppermute | solution.py:20
  510.8 167.0 %collective-permute-start.4 = (f32[256,768]{1,0:T(8,128)}, f32[256,768]{1,0:T(8,128)S(1)}, u32[]{:S(2)}, u32[]{:S(2)}) collective-permute-start(f32[256,768]{1,0:T(8,128)} %get-tuple-element.9), channel_id=1, source_target_pairs={{0,16},{16,32},{32,48},{48,64},{64,80},{80,96},{96,112},{112,128},... | collective-permute-start | bytes 2359304 | tf_op jit(solution)/shard_map/ppermute | solution.py:20
  674.8 11.7 %collective-permute-start.5 = (f32[256,768]{1,0:T(8,128)S(1)}, f32[256,768]{1,0:T(8,128)}, u32[]{:S(2)}, u32[]{:S(2)}) collective-permute-start(f32[256,768]{1,0:T(8,128)S(1)} %get-tuple-element.10), channel_id=1, source_target_pairs={{0,16},{16,32},{32,48},{48,64},{64,80},{80,96},{96,112},{112,128},... | collective-permute-start | bytes 2359304 | tf_op jit(solution)/shard_map/ppermute | solution.py:20
  688.0 108.1 %collective-permute-start.6 = (f32[256,768]{1,0:T(8,128)S(1)}, f32[256,768]{1,0:T(8,128)S(1)}, u32[]{:S(2)}, u32[]{:S(2)}) collective-permute-start(f32[256,768]{1,0:T(8,128)S(1)} %get-tuple-element.4), channel_id=1, source_target_pairs={{0,464},{16,480},{32,496},{48,0},{64,16},{80,32},{96,48},{112,64},... | collective-permute-start | bytes 2359304 | tf_op jit(solution)/shard_map/ppermute | solution.py:20
  693.3 116.8 %collective-permute-start.7 = (f32[256,768]{1,0:T(8,128)S(1)}, f32[256,768]{1,0:T(8,128)S(1)}, u32[]{:S(2)}, u32[]{:S(2)}) collective-permute-start(f32[256,768]{1,0:T(8,128)S(1)} %get-tuple-element.6), channel_id=1, source_target_pairs={{0,464},{16,480},{32,496},{48,0},{64,16},{80,32},{96,48},{112,64},... | collective-permute-start | bytes 2359304 | tf_op jit(solution)/shard_map/ppermute | solution.py:20
Sparse Core Ops, SparseCore 0:
  14.3 164.7 all-gather.12
  181.8 144.0 all-gather.14
  328.0 161.2 all-gather.16
  491.8 175.5 all-gather.18
